TPU v7x, 256 devices: a whole 4x4x8 slice. The times are simulated.
256 devices in a mesh: atoms: 32 (over x_hi, z, core), grid: 8 (over y, x_lo).
Axes of the slice: x: 4 (x_hi: 2, x_lo: 2; x = x_hi * 2 + x_lo), y: 4, z: 8, core: 2. Of those that a mesh axis runs over, the one named last changes fastest.
Arguments:
- basis_values: bfloat16 [32, 8, 2048, 1152], P('atoms', 'grid'), may hold values from -6 to 6
- potential: float32 [32, 8, 2048], P('atoms', 'grid'), may hold values from -6 to 6
- block_lists: int32 [32, 8, 6], P('atoms', 'grid'), may hold values from -1 to 8, as said below
Outputs:
- density_columns: float32 [32, 8, 768, 128], P('atoms', 'grid')
Inputs may be any that keep to these rules, and one draw needn't show every extreme that they name: `block_lists`: entry 0 of every cell's list is 4, the cell itself. For some m from 4 to 6, entries 1 to m - 1 are distinct codes other than 4 whose neighbour cell lies on the line (line positions 0 to 7), and entries from m on are -1. Some cell has m = 6.
All inputs are finite; a program needn't handle non-finite values.
Results may differ from a plain program's by a relative error of at most 0.0017.
Values sent between devices are 32-bit elements; how exact they have to be, the bound alone decides.
A program may use at most 64 MiB of HBM per device.

v0:
```python
import jax
import jax.numpy as jnp
from jax import lax
from jax.experimental import pallas as pl
from jax.experimental.pallas import tpu as pltpu
from jax.sharding import PartitionSpec as P

MAXB = 6
B = 128
MESH = pl.DeviceIdType.MESH
F32 = jnp.float32
BF16 = jnp.bfloat16

LEFT_ROWS, OWN_ROWS, RIGHT_ROWS, LEFT_PAIR, OWN_PAIR, WIDE_PAIR = 0, 6, 12, 18, 27, 36


def sym_index(i, j):
    return i * 3 + j - i * (i + 1) // 2


class PairType:
    def __init__(self, number, symmetric, base):
        self.number, self.symmetric, self.base = number, symmetric, base
        self.keys = [(i, j) for i in range(3) for j in range(3) if i <= j or not symmetric]
        self.down = [(1, 1), (0, 1)] + ([] if symmetric else [(1, 0)])
        self.up = [(1, 2)] + ([] if symmetric else [(2, 1)])

    def at(self, i, j):
        return sym_index(i, j) if self.symmetric else i * 3 + j


TYPES = [
    PairType(0, True, OWN_ROWS),
    PairType(1, False, OWN_PAIR),
    PairType(2, False, WIDE_PAIR),
]


def exchange_kernel(
    n_atoms, n_grid, values, potential, out,
    weighted, send_ll, send_rr, send_lc, q0, q1, q2,
    got_ll, got_rr, got_lc, got_down, got_up, got_mid, got_far_down, got_far_up, mid, far,
    send_sem, recv_sem,
):
    a = lax.axis_index("atoms")
    r = lax.axis_index("grid")
    left, right = lax.rem(a + n_atoms - 1, n_atoms), lax.rem(a + 1, n_atoms)
    below, above = jnp.maximum(r - 1, 0), jnp.minimum(r + 1, n_grid - 1)
    below2, above2 = jnp.maximum(r - 2, 0), jnp.minimum(r + 2, n_grid - 1)
    has_below, has_above = r >= 1, r < n_grid - 1
    has_below2, has_above2 = r >= 2, r < n_grid - 2

    barrier = pltpu.get_barrier_semaphore()
    for peer in (left, right):
        pl.semaphore_signal(barrier, inc=1, device_id=(peer, r), device_id_type=MESH)
    for exists, peer in ((has_below, below), (has_above, above), (has_below2, below2), (has_above2, above2)):
        @pl.when(exists)
        def _():
            pl.semaphore_signal(barrier, inc=1, device_id=(a, peer), device_id_type=MESH)
    peers = 2
    for exists in (has_below, has_above, has_below2, has_above2):
        peers = peers + jnp.where(exists, 1, 0)
    pl.semaphore_wait(barrier, peers)

    counter = [0]
    sent = []

    def copy(src, dst, device, exists=None, recv=None):
        n = counter[0]
        counter[0] += 1
        c = pltpu.make_async_remote_copy(
            src_ref=src, dst_ref=dst, send_sem=send_sem.at[n],
            recv_sem=recv_sem.at[n if recv is None else recv],
            device_id=device, device_id_type=MESH,
        )
        if exists is None:
            c.start()
        else:
            pl.when(exists)(c.start)
        sent.append((c, exists))
        return c, n

    def wait_for(c, exists=None):
        if exists is None:
            c.wait_recv()
        else:
            pl.when(exists)(c.wait_recv)

    def weigh(group):
        for part in range(4):
            rows = slice(part * 512, part * 512 + 512)
            turned = values[rows, group * 384:group * 384 + 384].T
            weighted[:, rows] = (turned.astype(F32) * potential[:, rows]).astype(BF16)

    def product(group, other, dst, symmetric):
        for i in range(3):
            first = i if symmetric else 0
            row = jnp.dot(
                weighted[i * B:i * B + B, :],
                values[:, other * 384 + first * B:other * 384 + 384],
                preferred_element_type=F32,
            )
            for j in range(first, 3):
                n = sym_index(i, j) if symmetric else i * 3 + j
                dst[n] = row[:, (j - first) * B:(j - first) * B + B]

    q = [q0, q1, q2]
    state = [dict() for _ in TYPES]

    def line_first(t):
        s, num, mine = state[t.number], t.number, q[t.number]
        s["fd"] = copy(mine.at[t.at(0, 0)], got_far_down.at[num], (a, below2), has_below2)
        s["down"] = [copy(mine.at[t.at(*key)], got_down.at[num * 3 + n], (a, below), has_below) for n, key in enumerate(t.down)]
        s["up"] = [copy(mine.at[t.at(*key)], got_up.at[num * 2 + n], (a, above), has_above) for n, key in enumerate(t.up)]

    def line_second(t):
        s, num, mine = state[t.number], t.number, q[t.number]
        wait_for(s["fd"][0], has_above2)
        mid[num] = mine[t.at(2, 2)] + got_far_down[num]
        s["mid"] = copy(mid.at[num], got_mid.at[num], (a, above), has_above)
        copy(mine.at[t.at(0, 0)], got_mid.at[num], (a, below), r == 1, s["mid"][1])
        wait_for(s["down"][0][0], has_above)
        far[num] = mine[t.at(2, 2)] + got_down[num * 3]
        s["fu"] = copy(far.at[num], got_far_up.at[num], (a, above2), has_above2)
        copy(mine.at[t.at(1, 1)], got_far_up.at[num], (a, above), r == 0, s["fu"][1])

    def line_last(t, done):
        s, num, mine = state[t.number], t.number, q[t.number]

        def put(key, value):
            out[t.base + t.at(*key)] = value
            done(t.at(*key))

        put((0, 2), mine[t.at(0, 2)])
        if not t.symmetric:
            put((2, 0), mine[t.at(2, 0)])
        put((2, 2), far[num] + got_far_down[num])
        for n, (i, j) in list(enumerate(t.down))[1:]:
            wait_for(s["down"][n][0], has_above)
            put((i + 1, j + 1), mine[t.at(i + 1, j + 1)] + got_down[num * 3 + n])
        for n, (i, j) in enumerate(t.up):
            wait_for(s["up"][n][0], has_below)
            put((i - 1, j - 1), mine[t.at(i - 1, j - 1)] + got_up[num * 2 + n])
        wait_for(s["mid"][0])
        put((1, 1), mine[t.at(1, 1)] + got_mid[num])
        wait_for(s["fu"][0], has_below)
        put((0, 0), mine[t.at(0, 0)] + got_far_up[num])

    t0, t1, t2 = TYPES
    zero = jnp.zeros((B, B), F32)

    @pl.when(jnp.logical_not(has_above2))
    def _():
        for num in range(3):
            got_far_down[num] = zero

    weigh(0)
    product(0, 2, q2, False)
    line_first(t2)
    product(0, 1, send_lc, False)
    lc = [copy(send_lc.at[n], got_lc.at[n], (left, r)) for n in range(9)]
    product(0, 0, send_ll, True)
    ll = [copy(send_ll.at[n], got_ll.at[n], (left, r)) for n in range(6)]
    weigh(2)
    product(2, 2, send_rr, True)
    rr = [copy(send_rr.at[n], got_rr.at[n], (right, r)) for n in range(6)]
    weigh(1)
    product(1, 2, q1, False)
    product(1, 1, q0, True)
    line_second(t2)
    for n in range(9):
        wait_for(lc[n][0])
        q1[n] = q1[n] + got_lc[n]
    line_first(t1)
    for n in range(6):
        wait_for(ll[n][0])
        wait_for(rr[n][0])
        q0[n] = q0[n] + got_ll[n] + got_rr[n]
    line_first(t0)
    line_second(t1)
    line_second(t0)
    arrivals = []

    def pass_pair(n):
        arrivals.append(copy(out.at[OWN_PAIR + n], out.at[LEFT_PAIR + n], (right, r)))

    def pass_rows(n):
        arrivals.append(copy(out.at[OWN_ROWS + n], out.at[RIGHT_ROWS + n], (left, r)))
        arrivals.append(copy(out.at[OWN_ROWS + n], out.at[LEFT_ROWS + n], (right, r)))

    line_last(t2, lambda n: None)
    line_last(t1, pass_pair)
    line_last(t0, pass_rows)
    for c, _ in arrivals:
        c.wait_recv()
    for c, exists in sent:
        if exists is None:
            c.wait_send()
        else:
            pl.when(exists)(c.wait_send)


COPIES = 21 + 3 * 4 + (2 + 1) + 2 * (3 + 2) + 21 + 6


def exchange(values, potential, n_atoms, n_grid):
    def blocks(n):
        return pltpu.VMEM((n, B, B), F32)

    vmem = pl.BlockSpec(memory_space=pltpu.VMEM)
    return pl.pallas_call(
        lambda *refs: exchange_kernel(n_atoms, n_grid, *refs),
        out_shape=jax.ShapeDtypeStruct((45, B, B), F32),
        in_specs=[vmem, vmem],
        out_specs=vmem,
        scratch_shapes=[
            pltpu.VMEM((3 * B, values.shape[0]), BF16),
            blocks(6), blocks(6), blocks(9), blocks(6), blocks(9), blocks(9),
            blocks(6), blocks(6), blocks(9), blocks(9), blocks(6), blocks(3), blocks(3), blocks(3), blocks(3), blocks(3),
            pltpu.SemaphoreType.DMA((COPIES,)),
            pltpu.SemaphoreType.DMA((COPIES,)),
        ],
        compiler_params=pltpu.CompilerParams(
            collective_id=0, has_side_effects=True, vmem_limit_bytes=48 << 20
        ),
        name="exchange",
    )(values, potential)


def split(x):
    high = x.astype(BF16)
    return high, (x - high.astype(F32)).astype(BF16)


def sign_kernel(codes, blocks, out, raw, nh, nl, sh, sl, xh, xl, x):
    n = MAXB * B
    live = jnp.int32(0)
    for s in range(MAXB):
        live = live + jnp.where(codes[s] >= 0, 1, 0)

    def block_of(first, second):
        a1, i = first // 3, lax.rem(first, 3)
        a2, j = second // 3, lax.rem(second, 3)
        same = 6 * a1 + i * 3 + j - i * (i + 1) // 2
        apart = jnp.where(a2 - a1 == 2, WIDE_PAIR, LEFT_PAIR + 9 * a1) + i * 3 + j
        return jnp.where(a1 == a2, same, apart)

    eye = lax.broadcasted_iota(jnp.int32, (B, B), 0) == lax.broadcasted_iota(jnp.int32, (B, B), 1)
    zero = jnp.zeros((B, B), F32)
    trace = jnp.zeros((1, 1), F32)
    for s in range(MAXB):
        for t in range(s, MAXB):
            cs, ct = jnp.maximum(codes[s], 0), jnp.maximum(codes[t], 0)
            used = codes[t] >= 0
            blk = jnp.where(used, blocks[block_of(jnp.minimum(cs, ct), jnp.maximum(cs, ct))], zero)
            if s == t:
                raw[s * B:s * B + B, s * B:s * B + B] = blk
                trace = trace + jnp.sum(jnp.where(eye, blk, 0.0), keepdims=True)
            else:
                turned = blk.T
                ordered = cs < ct
                raw[s * B:s * B + B, t * B:t * B + B] = jnp.where(ordered, blk, turned)
                raw[t * B:t * B + B, s * B:s * B + B] = jnp.where(ordered, turned, blk)
    count = jnp.full((1, 1), live * B, jnp.int32).astype(F32)
    mean = trace / count
    total = jnp.zeros((1, 1), F32)
    for s in range(MAXB):
        rows = slice(s * B, s * B + B)
        diagonal = jnp.where(eye, jnp.where(s < live, mean, 0.0), 0.0)
        raw[rows, rows] = raw[rows, rows] - diagonal
        part = raw[rows, :]
        total = total + jnp.sum(part * part, keepdims=True)
    scale = -lax.rsqrt(total + 1e-06) * jnp.sqrt(count)
    for s in range(MAXB):
        rows = slice(s * B, s * B + B)
        part = raw[rows, :] * scale
        raw[rows, :] = part
        nh[rows, :], nl[rows, :] = split(part)

    tall = 256

    def dot(p, q):
        return jnp.dot(p, q, preferred_element_type=F32)

    def dot3(ph, plo, rows, qh, qlo):
        return dot(ph[rows, :], qh[...]) + (dot(ph[rows, :], qlo[...]) + dot(plo[rows, :], qh[...]))

    def rows_of(i):
        return pl.ds(pl.multiple_of(i * tall, tall), tall)

    @pl.loop(0, n // tall)
    def _(i):
        rows = rows_of(i)
        sh[rows, :], sl[rows, :] = split(dot3(nh, nl, rows, nh, nl))

    def fourth(i, acc):
        f = dot(sh[rows_of(i), :], sh[...])
        return acc + jnp.sum(f * f, keepdims=True)

    norm = lax.fori_loop(0, n // tall, fourth, jnp.zeros((1, 1), F32))
    rho = jnp.sqrt(jnp.sqrt(jnp.sqrt(norm + 1e-06)))
    inverse = 1.0 / rho
    linear, cubic = 1.5 * inverse, 0.5 * inverse * inverse * inverse

    @pl.loop(0, n // tall)
    def _(i):
        rows = rows_of(i)
        new = linear * raw[rows, :] - cubic * dot3(nh, nl, rows, sh, sl)
        x[rows, :] = new
        xh[rows, :], xl[rows, :] = split(new)

    @pl.loop(0, n // tall)
    def _(i):
        rows = rows_of(i)
        sh[rows, :], sl[rows, :] = split(dot3(xh, xl, rows, xh, xl))

    @pl.loop(0, n // tall)
    def _(i):
        rows = rows_of(i)
        new = 1.5 * x[rows, :] - 0.5 * dot3(xh, xl, rows, sh, sl)
        raw[rows, :] = new
        nh[rows, :], nl[rows, :] = split(new)

    @pl.loop(0, n // tall)
    def _(i):
        rows = rows_of(i)
        sh[rows, :B], sl[rows, :B] = split(dot3(nh, nl, rows, nh.at[:, :B], nl.at[:, :B]))

    for i in range(n // tall):
        rows = slice(i * tall, i * tall + tall)
        sign = 1.5 * raw[rows, :B] - 0.5 * dot3(nh, nl, rows, sh.at[:, :B], sl.at[:, :B])
        if i == 0:
            at = lax.broadcasted_iota(jnp.int32, (tall, B), 0) == lax.broadcasted_iota(jnp.int32, (tall, B), 1)
            sign = sign + jnp.where(at, 1.0, 0.0)
        out[rows, :] = 0.5 * sign


def sign_columns(codes, blocks):
    n = MAXB * B
    vmem = pl.BlockSpec(memory_space=pltpu.VMEM)
    half = pltpu.VMEM((n, n), BF16)
    full = pltpu.VMEM((n, n), F32)
    return pl.pallas_call(
        sign_kernel,
        out_shape=jax.ShapeDtypeStruct((n, B), F32),
        in_specs=[pl.BlockSpec(memory_space=pltpu.SMEM), vmem],
        out_specs=vmem,
        scratch_shapes=[full, half, half, half, half, half, half, full],
        compiler_params=pltpu.CompilerParams(vmem_limit_bytes=40 << 20),
        name="sign_columns",
    )(codes, blocks)


def solution(mesh):
    n_atoms, n_grid = mesh.shape["atoms"], mesh.shape["grid"]

    def shards(basis_values, potential, block_lists):
        blocks = exchange(basis_values[0, 0], potential[0], n_atoms, n_grid)
        return sign_columns(block_lists[0, 0], blocks)[None, None]

    placed = (P("atoms", "grid", None, None), P("atoms", "grid", None), P("atoms", "grid", None))
    return jax.shard_map(
        shards, mesh=mesh, in_specs=placed, out_specs=P("atoms", "grid", None, None), check_vma=False
    )
```

profile of v0, /device:TPU:8, one launch (start us, length us, event | category | flops | bytes accessed | tf_op | source)
XLA Modules:
  0.0 81.1 jit_solution(17840764183268057919)
XLA Ops:
  0.0 0.0 copy-start.1
  0.0 0.0 copy-start
  0.0 0.7 copy-done
  0.7 59.1 %exchange.1.blocks = f32[45,128,128]{2,1,0:T(8,128)S(1)} custom-call(bf16[2048,1152]{1,0:T(8,128)(2,1)} %bitcast.6, f32[1,2048]{1,0:T(1,128)S(1)} %bitcast.4), custom_call_target="tpu_custom_call" | custom-call | tf_op jit(solution)/shard_map/exchange/pallas_call | solution.py:211
  59.8 0.0 copy-done.1
  59.8 21.3 %sign_columns.1 = f32[768,128]{1,0:T(8,128)} custom-call(s32[6]{0:T(128)S(1)} %bitcast.5, f32[45,128,128]{2,1,0:T(8,128)S(1)} %exchange.1.blocks), custom_call_target="tpu_custom_call" | custom-call | tf_op jit(solution)/shard_map/sign_columns/pallas_call | solution.py:343
Async XLA Ops:
  0.0 59.8 %copy-start.1 = (s32[1,1,6]{2,1,0:T(1,128)S(1)}, s32[1,1,6]{2,1,0:T(1,128)}, u32[]{:S(2)}) copy-start(s32[1,1,6]{2,1,0:T(1,128)} %param.5) | copy-start | bytes 76
  0.0 0.7 copy-start
where the time goes:
time: 81.2 us; the launch traced here: 81.1 us
  Pallas kernels  80.3 us (99%)
    pallas_call x1, Pallas kernels, exchange(): pl.pallas_call(lambda *refs: exchange_kernel(n_atoms, n_grid, *refs), out...  59.1 us
    pallas_call x1, Pallas kernels, sign_columns(): pl.pallas_call(sign_kernel, out_shape=jax.ShapeDtypeStruct((n, B), F32),...  21.3 us

commit v1 on v0

--- a/solution.py
+++ b/solution.py
@@ -227,12 +227,7 @@
     )(values, potential)
 
 
-def split(x):
-    high = x.astype(BF16)
-    return high, (x - high.astype(F32)).astype(BF16)
-
-
-def sign_kernel(codes, blocks, out, raw, nh, nl, sh, sl, xh, xl, x):
+def sign_kernel(codes, blocks, out, raw, low, square, x):
     n = MAXB * B
     live = jnp.int32(0)
     for s in range(MAXB):
@@ -247,88 +242,70 @@
 
     eye = lax.broadcasted_iota(jnp.int32, (B, B), 0) == lax.broadcasted_iota(jnp.int32, (B, B), 1)
     zero = jnp.zeros((B, B), F32)
-    trace = jnp.zeros((1, 1), F32)
+    diagonal = jnp.zeros((B, B), F32)
+    for s in range(MAXB):
+        cs = jnp.maximum(codes[s], 0)
+        diagonal = diagonal + jnp.where(codes[s] >= 0, blocks[block_of(cs, cs)], zero)
+    trace = jnp.sum(jnp.where(eye, diagonal, zero), keepdims=True)
+    count = jnp.full((1, 1), live * B, jnp.int32).astype(F32)
+    mean = trace / count
+    once, twice = zero, zero
     for s in range(MAXB):
         for t in range(s, MAXB):
             cs, ct = jnp.maximum(codes[s], 0), jnp.maximum(codes[t], 0)
             used = codes[t] >= 0
             blk = jnp.where(used, blocks[block_of(jnp.minimum(cs, ct), jnp.maximum(cs, ct))], zero)
+            rows, cols = slice(s * B, s * B + B), slice(t * B, t * B + B)
             if s == t:
-                raw[s * B:s * B + B, s * B:s * B + B] = blk
-                trace = trace + jnp.sum(jnp.where(eye, blk, 0.0), keepdims=True)
+                blk = blk - jnp.where(eye, jnp.where(used, mean, 0.0), zero)
+                once = once + blk * blk
+                raw[rows, cols] = blk
+                low[rows, cols] = blk.astype(BF16)
             else:
                 turned = blk.T
+                twice = twice + blk * blk
                 ordered = cs < ct
-                raw[s * B:s * B + B, t * B:t * B + B] = jnp.where(ordered, blk, turned)
-                raw[t * B:t * B + B, s * B:s * B + B] = jnp.where(ordered, turned, blk)
-    count = jnp.full((1, 1), live * B, jnp.int32).astype(F32)
-    mean = trace / count
-    total = jnp.zeros((1, 1), F32)
-    for s in range(MAXB):
-        rows = slice(s * B, s * B + B)
-        diagonal = jnp.where(eye, jnp.where(s < live, mean, 0.0), 0.0)
-        raw[rows, rows] = raw[rows, rows] - diagonal
-        part = raw[rows, :]
-        total = total + jnp.sum(part * part, keepdims=True)
+                here, there = jnp.where(ordered, blk, turned), jnp.where(ordered, turned, blk)
+                raw[rows, cols] = here
+                raw[cols, rows] = there
+                low[rows, cols] = here.astype(BF16)
+                low[cols, rows] = there.astype(BF16)
+    total = jnp.sum(once + 2.0 * twice, keepdims=True)
     scale = -lax.rsqrt(total + 1e-06) * jnp.sqrt(count)
-    for s in range(MAXB):
-        rows = slice(s * B, s * B + B)
-        part = raw[rows, :] * scale
-        raw[rows, :] = part
-        nh[rows, :], nl[rows, :] = split(part)
-
     tall = 256
+    bands = [slice(i * tall, i * tall + tall) for i in range(n // tall)]
 
     def dot(p, q):
         return jnp.dot(p, q, preferred_element_type=F32)
 
-    def dot3(ph, plo, rows, qh, qlo):
-        return dot(ph[rows, :], qh[...]) + (dot(ph[rows, :], qlo[...]) + dot(plo[rows, :], qh[...]))
-
-    def rows_of(i):
-        return pl.ds(pl.multiple_of(i * tall, tall), tall)
-
-    @pl.loop(0, n // tall)
-    def _(i):
-        rows = rows_of(i)
-        sh[rows, :], sl[rows, :] = split(dot3(nh, nl, rows, nh, nl))
-
-    def fourth(i, acc):
-        f = dot(sh[rows_of(i), :], sh[...])
-        return acc + jnp.sum(f * f, keepdims=True)
-
-    norm = lax.fori_loop(0, n // tall, fourth, jnp.zeros((1, 1), F32))
+    for rows in bands:
+        square[rows, :] = (scale * scale * dot(low[rows, :], low[...])).astype(BF16)
+    norm = jnp.zeros((1, 1), F32)
+    for i, rows in enumerate(bands):
+        f = dot(square[rows, :], square[:, i * tall:])
+        norm = norm + jnp.sum(f[:, :tall] * f[:, :tall], keepdims=True)
+        if i + 1 < len(bands):
+            norm = norm + 2.0 * jnp.sum(f[:, tall:] * f[:, tall:], keepdims=True)
     rho = jnp.sqrt(jnp.sqrt(jnp.sqrt(norm + 1e-06)))
     inverse = 1.0 / rho
-    linear, cubic = 1.5 * inverse, 0.5 * inverse * inverse * inverse
-
-    @pl.loop(0, n // tall)
-    def _(i):
-        rows = rows_of(i)
-        new = linear * raw[rows, :] - cubic * dot3(nh, nl, rows, sh, sl)
+    linear, cubic = 1.5 * inverse * scale, 0.5 * inverse * inverse * inverse * scale
+    for rows in bands:
+        new = linear * raw[rows, :] - cubic * dot(low[rows, :], square[...])
         x[rows, :] = new
-        xh[rows, :], xl[rows, :] = split(new)
-
-    @pl.loop(0, n // tall)
-    def _(i):
-        rows = rows_of(i)
-        sh[rows, :], sl[rows, :] = split(dot3(xh, xl, rows, xh, xl))
-
-    @pl.loop(0, n // tall)
-    def _(i):
-        rows = rows_of(i)
-        new = 1.5 * x[rows, :] - 0.5 * dot3(xh, xl, rows, sh, sl)
-        raw[rows, :] = new
-        nh[rows, :], nl[rows, :] = split(new)
-
-    @pl.loop(0, n // tall)
-    def _(i):
-        rows = rows_of(i)
-        sh[rows, :B], sl[rows, :B] = split(dot3(nh, nl, rows, nh.at[:, :B], nl.at[:, :B]))
-
-    for i in range(n // tall):
-        rows = slice(i * tall, i * tall + tall)
-        sign = 1.5 * raw[rows, :B] - 0.5 * dot3(nh, nl, rows, sh.at[:, :B], sl.at[:, :B])
+    for rows in bands:
+        low[rows, :] = x[rows, :].astype(BF16)
+    for rows in bands:
+        square[rows, :] = dot(low[rows, :], low[...]).astype(BF16)
+    for rows in bands:
+        new = 1.5 * x[rows, :] - 0.5 * dot(low[rows, :], square[...])
+        raw[rows, :B] = new[:, :B]
+        x[rows, :] = new
+    for rows in bands:
+        low[rows, :] = x[rows, :].astype(BF16)
+    for rows in bands:
+        square[rows, :B] = dot(low[rows, :], low[:, :B]).astype(BF16)
+    for i, rows in enumerate(bands):
+        sign = 1.5 * raw[rows, :B] - 0.5 * dot(low[rows, :], square[:, :B])
         if i == 0:
             at = lax.broadcasted_iota(jnp.int32, (tall, B), 0) == lax.broadcasted_iota(jnp.int32, (tall, B), 1)
             sign = sign + jnp.where(at, 1.0, 0.0)
@@ -345,7 +322,7 @@
         out_shape=jax.ShapeDtypeStruct((n, B), F32),
         in_specs=[pl.BlockSpec(memory_space=pltpu.SMEM), vmem],
         out_specs=vmem,
-        scratch_shapes=[full, half, half, half, half, half, half, full],
+        scratch_shapes=[full, half, half, full],
         compiler_params=pltpu.CompilerParams(vmem_limit_bytes=40 << 20),
         name="sign_columns",
     )(codes, blocks)

time: 81.2 us -> 67.2 us (0.83)
  Pallas kernels: 80.3 us -> 66.3 us
    pallas_call x1, Pallas kernels: 21.3 us -> 7.28 us  [sign_columns(): pl.pallas_call(sign_kernel, out_shape=jax.ShapeDtypeStruct((n, B), F32),...]
where the time goes in v1:
time: 67.2 us; the launch traced here: 67.1 us
  Pallas kernels  66.3 us (99%)
  local copies, waits for them, and re-layouts  0.71 us (1%)
    pallas_call x1, Pallas kernels, exchange(): pl.pallas_call(lambda *refs: exchange_kernel(n_atoms, n_grid, *refs), out...  59.1 us
    pallas_call x1, Pallas kernels, sign_columns(): pl.pallas_call(sign_kernel, out_shape=jax.ShapeDtypeStruct((n, B), F32),...  7.28 us

profile of v1, /device:TPU:8, one launch (start us, length us, event | category | flops | bytes accessed | tf_op | source)
XLA Modules:
  0.0 67.1 jit_solution(13929644529126280371)
XLA Ops:
  0.0 0.0 copy-start.1
  0.0 0.0 copy-start
  0.0 0.7 %copy-done = f32[1,1,2048]{2,1,0:T(1,128)S(1)} copy-done((f32[1,1,2048]{2,1,0:T(1,128)S(1)}, f32[1,1,2048]{2,1,0:T(1,128)}, u32[]{:S(2)}) %copy-start) | copy-done | bytes 8216
  0.7 59.1 %exchange.1.blocks = f32[45,128,128]{2,1,0:T(8,128)S(1)} custom-call(bf16[2048,1152]{1,0:T(8,128)(2,1)} %bitcast.6, f32[1,2048]{1,0:T(1,128)S(1)} %bitcast.4), custom_call_target="tpu_custom_call" | custom-call | tf_op jit(solution)/shard_map/exchange/pallas_call | solution.py:211
  59.8 0.0 copy-done.1
  59.8 7.3 %sign_columns.1 = f32[768,128]{1,0:T(8,128)} custom-call(s32[6]{0:T(128)S(1)} %bitcast.5, f32[45,128,128]{2,1,0:T(8,128)S(1)} %exchange.1.blocks), custom_call_target="tpu_custom_call" | custom-call | tf_op jit(solution)/shard_map/sign_columns/pallas_call | solution.py:320
Async XLA Ops:
  0.0 59.8 %copy-start.1 = (s32[1,1,6]{2,1,0:T(1,128)S(1)}, s32[1,1,6]{2,1,0:T(1,128)}, u32[]{:S(2)}) copy-start(s32[1,1,6]{2,1,0:T(1,128)} %param.5) | copy-start | bytes 76
  0.0 0.7 %copy-start = (f32[1,1,2048]{2,1,0:T(1,128)S(1)}, f32[1,1,2048]{2,1,0:T(1,128)}, u32[]{:S(2)}) copy-start(f32[1,1,2048]{2,1,0:T(1,128)} %param.4) | copy-start | bytes 24580

commit v2 on v1

--- a/solution.py
+++ b/solution.py
@@ -39,57 +39,168 @@
 def exchange_kernel(
     n_atoms, n_grid, values, potential, out,
     weighted, send_ll, send_rr, send_lc, q0, q1, q2,
-    got_ll, got_rr, got_lc, got_down, got_up, got_mid, got_far_down, got_far_up, mid, far,
-    send_sem, recv_sem,
+    got_ll, got_rr, got_lc, got_down, got_up, got_mid, got_far_down, got_far_up, mid, far, v,
+    send_sem, recv_sem, load_sem,
 ):
+    loads = []
+    for n, group in enumerate((0, 2, 1)):
+        cols = slice(group * 384, group * 384 + 384)
+        loads.append(pltpu.make_async_copy(values.at[:, cols], v.at[:, cols], load_sem.at[n]))
+        loads[-1].start()
     a = lax.axis_index("atoms")
     r = lax.axis_index("grid")
+    last = n_grid - 1
+    half = n_atoms // 2
     left, right = lax.rem(a + n_atoms - 1, n_atoms), lax.rem(a + 1, n_atoms)
-    below, above = jnp.maximum(r - 1, 0), jnp.minimum(r + 1, n_grid - 1)
-    below2, above2 = jnp.maximum(r - 2, 0), jnp.minimum(r + 2, n_grid - 1)
-    has_below, has_above = r >= 1, r < n_grid - 1
-    has_below2, has_above2 = r >= 2, r < n_grid - 2
+    below, above = jnp.maximum(r - 1, 0), jnp.minimum(r + 1, last)
+    below2, above2 = jnp.maximum(r - 2, 0), jnp.minimum(r + 2, last)
+    has_below, has_above = r >= 1, r < last
+    has_below2, has_above2 = r >= 2, r < last - 1
+    odd = lax.rem(r, 2) == 1
+    even = jnp.logical_not(odd)
+    first_half, last_half = lax.rem(a, half) == 0, lax.rem(a, half) == half - 1
+    at_wrap = jnp.logical_or(first_half, last_half)
+    across = jnp.where(first_half, left, right)
 
     barrier = pltpu.get_barrier_semaphore()
     for peer in (left, right):
         pl.semaphore_signal(barrier, inc=1, device_id=(peer, r), device_id_type=MESH)
-    for exists, peer in ((has_below, below), (has_above, above), (has_below2, below2), (has_above2, above2)):
+    peers = 2
+    for exists, peer in (
+        (has_below, (a, below)), (has_above, (a, above)), (has_below2, (a, below2)), (has_above2, (a, above2)),
+        (jnp.logical_and(at_wrap, has_below), (across, below)), (jnp.logical_and(at_wrap, has_above), (across, above)),
+    ):
         @pl.when(exists)
         def _():
-            pl.semaphore_signal(barrier, inc=1, device_id=(a, peer), device_id_type=MESH)
-    peers = 2
-    for exists in (has_below, has_above, has_below2, has_above2):
+            pl.semaphore_signal(barrier, inc=1, device_id=peer, device_id_type=MESH)
         peers = peers + jnp.where(exists, 1, 0)
     pl.semaphore_wait(barrier, peers)
 
-    counter = [0]
+    next_send, next_recv = [0], [0]
     sent = []
 
-    def copy(src, dst, device, exists=None, recv=None):
-        n = counter[0]
-        counter[0] += 1
+    def receives(n):
+        next_recv[0] += n
+        return next_recv[0] - n
+
+    def when(condition, step):
+        if condition is None:
+            step()
+        else:
+            pl.when(condition)(step)
+
+    def copy(src, dst, device, exists, recv):
         c = pltpu.make_async_remote_copy(
-            src_ref=src, dst_ref=dst, send_sem=send_sem.at[n],
-            recv_sem=recv_sem.at[n if recv is None else recv],
+            src_ref=src, dst_ref=dst, send_sem=send_sem.at[next_send[0]], recv_sem=recv_sem.at[recv],
             device_id=device, device_id_type=MESH,
         )
-        if exists is None:
-            c.start()
-        else:
-            pl.when(exists)(c.start)
+        next_send[0] += 1
+        when(exists, c.start)
         sent.append((c, exists))
-        return c, n
-
-    def wait_for(c, exists=None):
-        if exists is None:
-            c.wait_recv()
-        else:
-            pl.when(exists)(c.wait_recv)
+
+    def arrival(dst, recv):
+        return pltpu.make_async_remote_copy(
+            src_ref=mid.at[0], dst_ref=dst, send_sem=send_sem.at[0], recv_sem=recv_sem.at[recv],
+            device_id=(right, r), device_id_type=MESH,
+        )
+
+    def valid(key):
+        low, high = min(key) > 0, max(key) < 2
+        if low and high:
+            return None
+        if low:
+            return has_above
+        return has_below if high else jnp.logical_and(has_below, has_above)
+
+    def choose(wrapped, ours, theirs):
+        ours = True if ours is None else ours
+        theirs = True if theirs is None else theirs
+        return jnp.logical_or(jnp.logical_and(wrapped, theirs), jnp.logical_and(jnp.logical_not(wrapped), ours))
+
+    def other(key):
+        if max(key) == 2 and min(key) == 0:
+            return key, r
+        if max(key) == 2:
+            return (key[0] - 1, key[1] - 1), above
+        return (key[0] + 1, key[1] + 1), below
+
+    class Reduce:
+        def __init__(self, src, got, t, peer, wrapped, receives_wrapped):
+            self.src, self.got, self.t, self.peer = src, got, t, peer
+            self.wrapped, self.receives_wrapped = wrapped, receives_wrapped
+            self.extra = len(t.keys)
+            self.recv = receives(self.extra + 1)
+
+        def send(self, key):
+            t = self.t
+            slot = t.at(*key)
+            if key == (1, 1):
+                theirs = jnp.where(even, t.at(0, 0), t.at(2, 2))
+                cell = jnp.where(even, above, below)
+            else:
+                moved, cell = other(key)
+                theirs = self.extra if key == (0, 0) else t.at(*moved)
+            to = jnp.where(self.wrapped, theirs, slot)
+            copy(
+                self.src.at[slot], self.got.at[to],
+                (self.peer, jnp.where(self.wrapped, cell, r)), valid(key), self.recv + to,
+            )
+
+        def add(self, key, q):
+            t = self.t
+            slot = t.at(*key)
+            ours = valid(key)
+            theirs = {(0, 0): odd, (2, 2): even, (1, 1): has_below}.get(key, ours)
+            arrives = ours if theirs is ours else choose(self.receives_wrapped, ours, theirs)
+
+            def step():
+                arrival(self.got.at[slot], self.recv + slot).wait_recv()
+                q[slot] = q[slot] + self.got[slot]
+
+            when(arrives, step)
+            if key == (1, 1):
+                @pl.when(jnp.logical_and(self.receives_wrapped, has_above))
+                def _():
+                    arrival(self.got.at[self.extra], self.recv + self.extra).wait_recv()
+                    q[slot] = q[slot] + self.got[self.extra]
+
+    class Gather:
+        def __init__(self, t, base, peer, wrapped):
+            self.t, self.base, self.peer, self.wrapped = t, base, peer, wrapped
+            self.recv = receives(len(t.keys))
+
+        def send(self, key):
+            t = self.t
+            src = out.at[t.base + t.at(*key)]
+
+            def go(slot, cell, exists):
+                copy(src, out.at[self.base + slot], (self.peer, cell), exists, self.recv + slot)
+
+            slot = t.at(*key)
+            if key == (1, 1):
+                go(
+                    jnp.where(self.wrapped, t.at(0, 0), slot), jnp.where(self.wrapped, above, r),
+                    choose(self.wrapped, None, has_above),
+                )
+                go(t.at(2, 2), below, jnp.logical_and(self.wrapped, has_below))
+                return
+            moved, cell = other(key)
+            ours = valid(key)
+            theirs = {(0, 0): odd, (2, 2): even}.get(key, ours)
+            go(
+                jnp.where(self.wrapped, t.at(*moved), slot), jnp.where(self.wrapped, cell, r),
+                ours if theirs is ours else choose(self.wrapped, ours, theirs),
+            )
+
+        def wait(self):
+            for key in self.t.keys:
+                slot = self.t.at(*key)
+                when(valid(key), arrival(out.at[self.base + slot], self.recv + slot).wait_recv)
 
     def weigh(group):
         for part in range(4):
             rows = slice(part * 512, part * 512 + 512)
-            turned = values[rows, group * 384:group * 384 + 384].T
+            turned = v[rows, group * 384:group * 384 + 384].T
             weighted[:, rows] = (turned.astype(F32) * potential[:, rows]).astype(BF16)
 
     def product(group, other, dst, symmetric):
@@ -97,7 +208,7 @@
             first = i if symmetric else 0
             row = jnp.dot(
                 weighted[i * B:i * B + B, :],
-                values[:, other * 384 + first * B:other * 384 + 384],
+                v[:, other * 384 + first * B:other * 384 + 384],
                 preferred_element_type=F32,
             )
             for j in range(first, 3):
@@ -105,102 +216,110 @@
                 dst[n] = row[:, (j - first) * B:(j - first) * B + B]
 
     q = [q0, q1, q2]
-    state = [dict() for _ in TYPES]
-
-    def line_first(t):
-        s, num, mine = state[t.number], t.number, q[t.number]
-        s["fd"] = copy(mine.at[t.at(0, 0)], got_far_down.at[num], (a, below2), has_below2)
-        s["down"] = [copy(mine.at[t.at(*key)], got_down.at[num * 3 + n], (a, below), has_below) for n, key in enumerate(t.down)]
-        s["up"] = [copy(mine.at[t.at(*key)], got_up.at[num * 2 + n], (a, above), has_above) for n, key in enumerate(t.up)]
-
-    def line_second(t):
-        s, num, mine = state[t.number], t.number, q[t.number]
-        wait_for(s["fd"][0], has_above2)
-        mid[num] = mine[t.at(2, 2)] + got_far_down[num]
-        s["mid"] = copy(mid.at[num], got_mid.at[num], (a, above), has_above)
-        copy(mine.at[t.at(0, 0)], got_mid.at[num], (a, below), r == 1, s["mid"][1])
-        wait_for(s["down"][0][0], has_above)
-        far[num] = mine[t.at(2, 2)] + got_down[num * 3]
-        s["fu"] = copy(far.at[num], got_far_up.at[num], (a, above2), has_above2)
-        copy(mine.at[t.at(1, 1)], got_far_up.at[num], (a, above), r == 0, s["fu"][1])
-
-    def line_last(t, done):
-        s, num, mine = state[t.number], t.number, q[t.number]
-
-        def put(key, value):
-            out[t.base + t.at(*key)] = value
-            done(t.at(*key))
-
-        put((0, 2), mine[t.at(0, 2)])
-        if not t.symmetric:
-            put((2, 0), mine[t.at(2, 0)])
-        put((2, 2), far[num] + got_far_down[num])
-        for n, (i, j) in list(enumerate(t.down))[1:]:
-            wait_for(s["down"][n][0], has_above)
-            put((i + 1, j + 1), mine[t.at(i + 1, j + 1)] + got_down[num * 3 + n])
-        for n, (i, j) in enumerate(t.up):
-            wait_for(s["up"][n][0], has_below)
-            put((i - 1, j - 1), mine[t.at(i - 1, j - 1)] + got_up[num * 2 + n])
-        wait_for(s["mid"][0])
-        put((1, 1), mine[t.at(1, 1)] + got_mid[num])
-        wait_for(s["fu"][0], has_below)
-        put((0, 0), mine[t.at(0, 0)] + got_far_up[num])
+
+    class Line:
+        def __init__(self, t, done):
+            self.t, self.done = t, done
+            self.recv = receives(8)
+
+        def first(self):
+            t, num, mine, recv = self.t, self.t.number, q[self.t.number], self.recv
+            copy(mine.at[t.at(0, 0)], got_far_down.at[num], (a, below2), has_below2, recv)
+            for n, key in enumerate(t.down):
+                copy(mine.at[t.at(*key)], got_down.at[num * 3 + n], (a, below), has_below, recv + 1 + n)
+            for n, key in enumerate(t.up):
+                copy(mine.at[t.at(*key)], got_up.at[num * 2 + n], (a, above), has_above, recv + 4 + n)
+            self.put((0, 2), mine[t.at(0, 2)])
+            if not t.symmetric:
+                self.put((2, 0), mine[t.at(2, 0)])
+
+        def second(self):
+            t, num, mine, recv = self.t, self.t.number, q[self.t.number], self.recv
+            when(has_above2, arrival(got_far_down.at[num], recv).wait_recv)
+            mid[num] = mine[t.at(2, 2)] + got_far_down[num]
+            copy(mid.at[num], got_mid.at[num], (a, above), has_above, recv + 6)
+            copy(mine.at[t.at(0, 0)], got_mid.at[num], (a, below), r == 1, recv + 6)
+            when(has_above, arrival(got_down.at[num * 3], recv + 1).wait_recv)
+            far[num] = mine[t.at(2, 2)] + got_down[num * 3]
+            copy(far.at[num], got_far_up.at[num], (a, above2), has_above2, recv + 7)
+            copy(mine.at[t.at(1, 1)], got_far_up.at[num], (a, above), r == 0, recv + 7)
+
+        def put(self, key, value):
+            out[self.t.base + self.t.at(*key)] = value
+            self.done(key)
+
+        def last(self):
+            t, num, mine, recv = self.t, self.t.number, q[self.t.number], self.recv
+            self.put((2, 2), far[num] + got_far_down[num])
+            for n, (i, j) in list(enumerate(t.down))[1:]:
+                when(has_above, arrival(got_down.at[num * 3 + n], recv + 1 + n).wait_recv)
+                self.put((i + 1, j + 1), mine[t.at(i + 1, j + 1)] + got_down[num * 3 + n])
+            for n, (i, j) in enumerate(t.up):
+                when(has_below, arrival(got_up.at[num * 2 + n], recv + 4 + n).wait_recv)
+                self.put((i - 1, j - 1), mine[t.at(i - 1, j - 1)] + got_up[num * 2 + n])
+            arrival(got_mid.at[num], recv + 6).wait_recv()
+            self.put((1, 1), mine[t.at(1, 1)] + got_mid[num])
+            when(has_below, arrival(got_far_up.at[num], recv + 7).wait_recv)
+            self.put((0, 0), mine[t.at(0, 0)] + got_far_up[num])
 
     t0, t1, t2 = TYPES
-    zero = jnp.zeros((B, B), F32)
+    pair_right = Gather(t1, LEFT_PAIR, right, last_half)
+    rows_right = Gather(t0, LEFT_ROWS, right, last_half)
+    rows_left = Gather(t0, RIGHT_ROWS, left, first_half)
+
+    def rows_done(key):
+        rows_right.send(key)
+        rows_left.send(key)
+
+    line0, line1, line2 = Line(t0, rows_done), Line(t1, pair_right.send), Line(t2, lambda key: None)
+    lc = Reduce(send_lc, got_lc, t1, left, first_half, last_half)
+    ll = Reduce(send_ll, got_ll, t0, left, first_half, last_half)
+    rr = Reduce(send_rr, got_rr, t0, right, last_half, first_half)
 
     @pl.when(jnp.logical_not(has_above2))
     def _():
         for num in range(3):
-            got_far_down[num] = zero
-
+            got_far_down[num] = jnp.zeros((B, B), F32)
+
+    loads[0].wait()
     weigh(0)
+    loads[1].wait()
     product(0, 2, q2, False)
-    line_first(t2)
+    line2.first()
+    loads[2].wait()
     product(0, 1, send_lc, False)
-    lc = [copy(send_lc.at[n], got_lc.at[n], (left, r)) for n in range(9)]
+    for key in t1.keys:
+        lc.send(key)
     product(0, 0, send_ll, True)
-    ll = [copy(send_ll.at[n], got_ll.at[n], (left, r)) for n in range(6)]
+    for key in t0.keys:
+        ll.send(key)
     weigh(2)
     product(2, 2, send_rr, True)
-    rr = [copy(send_rr.at[n], got_rr.at[n], (right, r)) for n in range(6)]
+    for key in t0.keys:
+        rr.send(key)
     weigh(1)
     product(1, 2, q1, False)
     product(1, 1, q0, True)
-    line_second(t2)
-    for n in range(9):
-        wait_for(lc[n][0])
-        q1[n] = q1[n] + got_lc[n]
-    line_first(t1)
-    for n in range(6):
-        wait_for(ll[n][0])
-        wait_for(rr[n][0])
-        q0[n] = q0[n] + got_ll[n] + got_rr[n]
-    line_first(t0)
-    line_second(t1)
-    line_second(t0)
-    arrivals = []
-
-    def pass_pair(n):
-        arrivals.append(copy(out.at[OWN_PAIR + n], out.at[LEFT_PAIR + n], (right, r)))
-
-    def pass_rows(n):
-        arrivals.append(copy(out.at[OWN_ROWS + n], out.at[RIGHT_ROWS + n], (left, r)))
-        arrivals.append(copy(out.at[OWN_ROWS + n], out.at[LEFT_ROWS + n], (right, r)))
-
-    line_last(t2, lambda n: None)
-    line_last(t1, pass_pair)
-    line_last(t0, pass_rows)
-    for c, _ in arrivals:
-        c.wait_recv()
+    line2.second()
+    for key in t1.keys:
+        lc.add(key, q1)
+    line1.first()
+    for key in t0.keys:
+        ll.add(key, q0)
+        rr.add(key, q0)
+    line0.first()
+    line1.second()
+    line0.second()
+    line2.last()
+    line1.last()
+    line0.last()
+    for gather in (pair_right, rows_right, rows_left):
+        gather.wait()
     for c, exists in sent:
-        if exists is None:
-            c.wait_send()
-        else:
-            pl.when(exists)(c.wait_send)
-
-
-COPIES = 21 + 3 * 4 + (2 + 1) + 2 * (3 + 2) + 21 + 6
+        when(exists, c.wait_send)
+
+
+COPIES = 96
 
 
 def exchange(values, potential, n_atoms, n_grid):
@@ -211,14 +330,16 @@
     return pl.pallas_call(
         lambda *refs: exchange_kernel(n_atoms, n_grid, *refs),
         out_shape=jax.ShapeDtypeStruct((45, B, B), F32),
-        in_specs=[vmem, vmem],
+        in_specs=[pl.BlockSpec(memory_space=pl.ANY), vmem],
         out_specs=vmem,
         scratch_shapes=[
             pltpu.VMEM((3 * B, values.shape[0]), BF16),
             blocks(6), blocks(6), blocks(9), blocks(6), blocks(9), blocks(9),
-            blocks(6), blocks(6), blocks(9), blocks(9), blocks(6), blocks(3), blocks(3), blocks(3), blocks(3), blocks(3),
+            blocks(7), blocks(7), blocks(10), blocks(9), blocks(6), blocks(3), blocks(3), blocks(3), blocks(3), blocks(3),
+            pltpu.VMEM(values.shape, BF16),
             pltpu.SemaphoreType.DMA((COPIES,)),
             pltpu.SemaphoreType.DMA((COPIES,)),
+            pltpu.SemaphoreType.DMA((3,)),
         ],
         compiler_params=pltpu.CompilerParams(
             collective_id=0, has_side_effects=True, vmem_limit_bytes=48 << 20

time: 67.2 us -> 55.3 us (0.82)
  Pallas kernels: 66.3 us -> 54 us
    pallas_call x1, Pallas kernels: 59.1 us -> 46.7 us  [exchange(): pl.pallas_call(lambda *refs: exchange_kernel(n_atoms, n_grid, *refs), out...]
where the time goes in v2:
time: 55.3 us; the launch traced here: 54.7 us
  Pallas kernels  54 us (98%)
  local copies, waits for them, and re-layouts  0.71 us (1%)
    pallas_call x1, Pallas kernels, exchange(): pl.pallas_call(lambda *refs: exchange_kernel(n_atoms, n_grid, *refs), out...  46.7 us
    pallas_call x1, Pallas kernels, sign_columns(): pl.pallas_call(sign_kernel, out_shape=jax.ShapeDtypeStruct((n, B), F32),...  7.28 us

profile of v2, /device:TPU:8, one launch (start us, length us, event | category | flops | bytes accessed | tf_op | source)
XLA Modules:
  0.0 54.7 jit_solution(13375767376709830895)
XLA Ops:
  0.0 0.0 copy-start.1
  0.0 0.0 copy-start
  0.0 0.7 %copy-done = f32[1,1,2048]{2,1,0:T(1,128)S(1)} copy-done((f32[1,1,2048]{2,1,0:T(1,128)S(1)}, f32[1,1,2048]{2,1,0:T(1,128)}, u32[]{:S(2)}) %copy-start) | copy-done | bytes 8216
  0.7 46.7 %exchange.1.blocks = f32[45,128,128]{2,1,0:T(8,128)S(1)} custom-call(bf16[2048,1152]{1,0:T(8,128)(2,1)} %bitcast.6, f32[1,2048]{1,0:T(1,128)S(1)} %bitcast.4), custom_call_target="tpu_custom_call" | custom-call | tf_op jit(solution)/shard_map/exchange/pallas_call | solution.py:330
  47.4 0.0 copy-done.1
  47.4 7.3 %sign_columns.1 = f32[768,128]{1,0:T(8,128)} custom-call(s32[6]{0:T(128)S(1)} %bitcast.5, f32[45,128,128]{2,1,0:T(8,128)S(1)} %exchange.1.blocks), custom_call_target="tpu_custom_call" | custom-call | tf_op jit(solution)/shard_map/sign_columns/pallas_call | solution.py:441
Async XLA Ops:
  0.0 47.4 %copy-start.1 = (s32[1,1,6]{2,1,0:T(1,128)S(1)}, s32[1,1,6]{2,1,0:T(1,128)}, u32[]{:S(2)}) copy-start(s32[1,1,6]{2,1,0:T(1,128)} %param.5) | copy-start | bytes 76
  0.0 0.7 %copy-start = (f32[1,1,2048]{2,1,0:T(1,128)S(1)}, f32[1,1,2048]{2,1,0:T(1,128)}, u32[]{:S(2)}) copy-start(f32[1,1,2048]{2,1,0:T(1,128)} %param.4) | copy-start | bytes 24580

commit v3 on v2

--- a/solution.py
+++ b/solution.py
@@ -204,16 +204,11 @@
             weighted[:, rows] = (turned.astype(F32) * potential[:, rows]).astype(BF16)
 
     def product(group, other, dst, symmetric):
+        block = jnp.dot(weighted[...], v[:, other * 384:other * 384 + 384], preferred_element_type=F32)
         for i in range(3):
-            first = i if symmetric else 0
-            row = jnp.dot(
-                weighted[i * B:i * B + B, :],
-                v[:, other * 384 + first * B:other * 384 + 384],
-                preferred_element_type=F32,
-            )
-            for j in range(first, 3):
+            for j in range(i if symmetric else 0, 3):
                 n = sym_index(i, j) if symmetric else i * 3 + j
-                dst[n] = row[:, (j - first) * B:(j - first) * B + B]
+                dst[n] = block[i * B:i * B + B, j * B:j * B + B]
 
     q = [q0, q1, q2]
 
@@ -222,43 +217,59 @@
             self.t, self.done = t, done
             self.recv = receives(8)
 
-        def first(self):
-            t, num, mine, recv = self.t, self.t.number, q[self.t.number], self.recv
-            copy(mine.at[t.at(0, 0)], got_far_down.at[num], (a, below2), has_below2, recv)
-            for n, key in enumerate(t.down):
-                copy(mine.at[t.at(*key)], got_down.at[num * 3 + n], (a, below), has_below, recv + 1 + n)
-            for n, key in enumerate(t.up):
-                copy(mine.at[t.at(*key)], got_up.at[num * 2 + n], (a, above), has_above, recv + 4 + n)
-            self.put((0, 2), mine[t.at(0, 2)])
-            if not t.symmetric:
-                self.put((2, 0), mine[t.at(2, 0)])
-
-        def second(self):
+        def start(self, key):
+            t, num, mine, recv = self.t, self.t.number, q[self.t.number], self.recv
+            src = mine.at[t.at(*key)]
+            if key == (0, 0):
+                copy(src, got_far_down.at[num], (a, below2), has_below2, recv)
+                copy(src, got_mid.at[num], (a, below), r == 1, recv + 6)
+            if key in t.down:
+                n = t.down.index(key)
+                copy(src, got_down.at[num * 3 + n], (a, below), has_below, recv + 1 + n)
+            if key in t.up:
+                n = t.up.index(key)
+                copy(src, got_up.at[num * 2 + n], (a, above), has_above, recv + 4 + n)
+            if key == (1, 1):
+                copy(src, got_far_up.at[num], (a, above), r == 0, recv + 7)
+            if key in ((0, 2), (2, 0)):
+                self.put(key, src[...])
+
+        def send_mid(self):
             t, num, mine, recv = self.t, self.t.number, q[self.t.number], self.recv
             when(has_above2, arrival(got_far_down.at[num], recv).wait_recv)
             mid[num] = mine[t.at(2, 2)] + got_far_down[num]
             copy(mid.at[num], got_mid.at[num], (a, above), has_above, recv + 6)
-            copy(mine.at[t.at(0, 0)], got_mid.at[num], (a, below), r == 1, recv + 6)
+
+        def send_far(self):
+            t, num, mine, recv = self.t, self.t.number, q[self.t.number], self.recv
             when(has_above, arrival(got_down.at[num * 3], recv + 1).wait_recv)
             far[num] = mine[t.at(2, 2)] + got_down[num * 3]
             copy(far.at[num], got_far_up.at[num], (a, above2), has_above2, recv + 7)
-            copy(mine.at[t.at(1, 1)], got_far_up.at[num], (a, above), r == 0, recv + 7)
 
         def put(self, key, value):
             out[self.t.base + self.t.at(*key)] = value
             self.done(key)
 
-        def last(self):
-            t, num, mine, recv = self.t, self.t.number, q[self.t.number], self.recv
-            self.put((2, 2), far[num] + got_far_down[num])
+        def sides(self):
+            t, num, mine, recv = self.t, self.t.number, q[self.t.number], self.recv
             for n, (i, j) in list(enumerate(t.down))[1:]:
                 when(has_above, arrival(got_down.at[num * 3 + n], recv + 1 + n).wait_recv)
                 self.put((i + 1, j + 1), mine[t.at(i + 1, j + 1)] + got_down[num * 3 + n])
             for n, (i, j) in enumerate(t.up):
                 when(has_below, arrival(got_up.at[num * 2 + n], recv + 4 + n).wait_recv)
                 self.put((i - 1, j - 1), mine[t.at(i - 1, j - 1)] + got_up[num * 2 + n])
+
+        def high(self):
+            t, num = self.t, self.t.number
+            self.put((2, 2), far[num] + got_far_down[num])
+
+        def centre(self):
+            t, num, mine, recv = self.t, self.t.number, q[self.t.number], self.recv
             arrival(got_mid.at[num], recv + 6).wait_recv()
             self.put((1, 1), mine[t.at(1, 1)] + got_mid[num])
+
+        def low(self):
+            t, num, mine, recv = self.t, self.t.number, q[self.t.number], self.recv
             when(has_below, arrival(got_far_up.at[num], recv + 7).wait_recv)
             self.put((0, 0), mine[t.at(0, 0)] + got_far_up[num])
 
@@ -281,38 +292,54 @@
         for num in range(3):
             got_far_down[num] = jnp.zeros((B, B), F32)
 
+    def in_order(t):
+        return [key for key in ((0, 0), (1, 1), (0, 1), (1, 0), (1, 2), (2, 1), (2, 2), (0, 2), (2, 0)) if key in t.keys]
+
     loads[0].wait()
     weigh(0)
     loads[1].wait()
     product(0, 2, q2, False)
-    line2.first()
+    for key in in_order(t2):
+        line2.start(key)
+    product(0, 0, send_ll, True)
+    for key in in_order(t0):
+        ll.send(key)
     loads[2].wait()
     product(0, 1, send_lc, False)
-    for key in t1.keys:
+    for key in in_order(t1):
         lc.send(key)
-    product(0, 0, send_ll, True)
-    for key in t0.keys:
-        ll.send(key)
     weigh(2)
     product(2, 2, send_rr, True)
-    for key in t0.keys:
+    for key in in_order(t0):
         rr.send(key)
     weigh(1)
+    product(1, 1, q0, True)
     product(1, 2, q1, False)
-    product(1, 1, q0, True)
-    line2.second()
-    for key in t1.keys:
-        lc.add(key, q1)
-    line1.first()
-    for key in t0.keys:
+    line2.send_far()
+    for key in in_order(t0):
         ll.add(key, q0)
         rr.add(key, q0)
-    line0.first()
-    line1.second()
-    line0.second()
-    line2.last()
-    line1.last()
-    line0.last()
+        line0.start(key)
+    for key in in_order(t1):
+        lc.add(key, q1)
+        line1.start(key)
+    line0.send_mid()
+    line0.send_far()
+    line1.send_mid()
+    line2.send_mid()
+    line0.sides()
+    line0.high()
+    line1.send_far()
+    line1.sides()
+    line1.high()
+    line0.centre()
+    line0.low()
+    line1.centre()
+    line1.low()
+    line2.sides()
+    line2.high()
+    line2.centre()
+    line2.low()
     for gather in (pair_right, rows_right, rows_left):
         gather.wait()
     for c, exists in sent:

time: 55.3 us -> 52.6 us (0.951)
  Pallas kernels: 54 us -> 51.2 us
    pallas_call x1, Pallas kernels: 46.7 us -> 44 us  [exchange(): pl.pallas_call(lambda *refs: exchange_kernel(n_atoms, n_grid, *refs), out...]
where the time goes in v3:
time: 52.6 us; the launch traced here: 52 us
  Pallas kernels  51.2 us (97%)
  local copies, waits for them, and re-layouts  0.71 us (1%)
    pallas_call x1, Pallas kernels, exchange(): pl.pallas_call(lambda *refs: exchange_kernel(n_atoms, n_grid, *refs), out...  44 us
    pallas_call x1, Pallas kernels, sign_columns(): pl.pallas_call(sign_kernel, out_shape=jax.ShapeDtypeStruct((n, B), F32),...  7.28 us

profile of v3, /device:TPU:8, one launch (start us, length us, event | category | flops | bytes accessed | tf_op | source)
XLA Modules:
  0.0 52.0 jit_solution(9135240877495695966)
XLA Ops:
  0.0 0.0 copy-start.1
  0.0 0.0 copy-start
  0.0 0.7 %copy-done = f32[1,1,2048]{2,1,0:T(1,128)S(1)} copy-done((f32[1,1,2048]{2,1,0:T(1,128)S(1)}, f32[1,1,2048]{2,1,0:T(1,128)}, u32[]{:S(2)}) %copy-start) | copy-done | bytes 8216
  0.7 44.0 %exchange.1.blocks = f32[45,128,128]{2,1,0:T(8,128)S(1)} custom-call(bf16[2048,1152]{1,0:T(8,128)(2,1)} %bitcast.6, f32[1,2048]{1,0:T(1,128)S(1)} %bitcast.4), custom_call_target="tpu_custom_call" | custom-call | tf_op jit(solution)/shard_map/exchange/pallas_call | solution.py:357
  44.7 0.0 copy-done.1
  44.7 7.3 %sign_columns.1 = f32[768,128]{1,0:T(8,128)} custom-call(s32[6]{0:T(128)S(1)} %bitcast.5, f32[45,128,128]{2,1,0:T(8,128)S(1)} %exchange.1.blocks), custom_call_target="tpu_custom_call" | custom-call | tf_op jit(solution)/shard_map/sign_columns/pallas_call | solution.py:468
Async XLA Ops:
  0.0 44.7 %copy-start.1 = (s32[1,1,6]{2,1,0:T(1,128)S(1)}, s32[1,1,6]{2,1,0:T(1,128)}, u32[]{:S(2)}) copy-start(s32[1,1,6]{2,1,0:T(1,128)} %param.5) | copy-start | bytes 76
  0.0 0.7 %copy-start = (f32[1,1,2048]{2,1,0:T(1,128)S(1)}, f32[1,1,2048]{2,1,0:T(1,128)}, u32[]{:S(2)}) copy-start(f32[1,1,2048]{2,1,0:T(1,128)} %param.4) | copy-start | bytes 24580

commit v4 on v3

--- a/solution.py
+++ b/solution.py
@@ -19,27 +19,32 @@
 
 
 class PairType:
-    def __init__(self, number, symmetric, base):
+    def __init__(self, number, symmetric, base, distances):
         self.number, self.symmetric, self.base = number, symmetric, base
-        self.keys = [(i, j) for i in range(3) for j in range(3) if i <= j or not symmetric]
-        self.down = [(1, 1), (0, 1)] + ([] if symmetric else [(1, 0)])
-        self.up = [(1, 2)] + ([] if symmetric else [(2, 1)])
+        self.size = 6 if symmetric else 9
+        self.keys = [
+            (i, j) for i in range(3) for j in range(3)
+            if abs(i - j) in distances and (i <= j or not symmetric)
+        ]
+        self.down = [key for key in ((1, 1), (0, 1), (1, 0)) if key in self.keys]
+        self.up = [key for key in ((1, 2), (2, 1)) if key in self.keys]
 
     def at(self, i, j):
         return sym_index(i, j) if self.symmetric else i * 3 + j
 
 
 TYPES = [
-    PairType(0, True, OWN_ROWS),
-    PairType(1, False, OWN_PAIR),
-    PairType(2, False, WIDE_PAIR),
+    PairType(0, True, OWN_ROWS, (0, 1, 2)),
+    PairType(1, False, OWN_PAIR, (0, 2)),
+    PairType(2, False, WIDE_PAIR, (0, 1, 2)),
+    PairType(3, False, LEFT_PAIR, (1,)),
 ]
 
 
 def exchange_kernel(
     n_atoms, n_grid, values, potential, out,
-    weighted, send_ll, send_rr, send_lc, q0, q1, q2,
-    got_ll, got_rr, got_lc, got_down, got_up, got_mid, got_far_down, got_far_up, mid, far, v,
+    weighted, send_ll, send_rr, send_lc, send_cr, q0, q1, q2, q3,
+    got_ll, got_rr, got_lc, got_cr, got_down, got_up, got_mid, got_far_down, got_far_up, mid, far, v,
     send_sem, recv_sem, load_sem,
 ):
     loads = []
@@ -74,7 +79,6 @@
         def _():
             pl.semaphore_signal(barrier, inc=1, device_id=peer, device_id_type=MESH)
         peers = peers + jnp.where(exists, 1, 0)
-    pl.semaphore_wait(barrier, peers)
 
     next_send, next_recv = [0], [0]
     sent = []
@@ -97,6 +101,13 @@
         next_send[0] += 1
         when(exists, c.start)
         sent.append((c, exists))
+        return sent[-1]
+
+    def flush(copies):
+        for entry in copies:
+            c, exists = entry
+            when(exists, c.wait_send)
+            sent[:] = [other for other in sent if other is not entry]
 
     def arrival(dst, recv):
         return pltpu.make_async_remote_copy(
@@ -128,7 +139,7 @@
         def __init__(self, src, got, t, peer, wrapped, receives_wrapped):
             self.src, self.got, self.t, self.peer = src, got, t, peer
             self.wrapped, self.receives_wrapped = wrapped, receives_wrapped
-            self.extra = len(t.keys)
+            self.extra = t.size
             self.recv = receives(self.extra + 1)
 
         def send(self, key):
@@ -167,7 +178,7 @@
     class Gather:
         def __init__(self, t, base, peer, wrapped):
             self.t, self.base, self.peer, self.wrapped = t, base, peer, wrapped
-            self.recv = receives(len(t.keys))
+            self.recv = receives(t.size)
 
         def send(self, key):
             t = self.t
@@ -203,14 +214,13 @@
             turned = v[rows, group * 384:group * 384 + 384].T
             weighted[:, rows] = (turned.astype(F32) * potential[:, rows]).astype(BF16)
 
-    def product(group, other, dst, symmetric):
+    def product(group, other, *places):
         block = jnp.dot(weighted[...], v[:, other * 384:other * 384 + 384], preferred_element_type=F32)
-        for i in range(3):
-            for j in range(i if symmetric else 0, 3):
-                n = sym_index(i, j) if symmetric else i * 3 + j
-                dst[n] = block[i * B:i * B + B, j * B:j * B + B]
-
-    q = [q0, q1, q2]
+        for t, dst in places:
+            for i, j in t.keys:
+                dst[t.at(i, j)] = block[i * B:i * B + B, j * B:j * B + B]
+
+    q = [q0, q1, q2, q3]
 
     class Line:
         def __init__(self, t, done):
@@ -220,25 +230,27 @@
         def start(self, key):
             t, num, mine, recv = self.t, self.t.number, q[self.t.number], self.recv
             src = mine.at[t.at(*key)]
+            started = []
             if key == (0, 0):
                 copy(src, got_far_down.at[num], (a, below2), has_below2, recv)
                 copy(src, got_mid.at[num], (a, below), r == 1, recv + 6)
             if key in t.down:
                 n = t.down.index(key)
-                copy(src, got_down.at[num * 3 + n], (a, below), has_below, recv + 1 + n)
+                started.append(copy(src, got_down.at[num * 3 + n], (a, below), has_below, recv + 1 + n))
             if key in t.up:
                 n = t.up.index(key)
-                copy(src, got_up.at[num * 2 + n], (a, above), has_above, recv + 4 + n)
+                started.append(copy(src, got_up.at[num * 2 + n], (a, above), has_above, recv + 4 + n))
             if key == (1, 1):
                 copy(src, got_far_up.at[num], (a, above), r == 0, recv + 7)
             if key in ((0, 2), (2, 0)):
                 self.put(key, src[...])
+            return started
 
         def send_mid(self):
             t, num, mine, recv = self.t, self.t.number, q[self.t.number], self.recv
             when(has_above2, arrival(got_far_down.at[num], recv).wait_recv)
             mid[num] = mine[t.at(2, 2)] + got_far_down[num]
-            copy(mid.at[num], got_mid.at[num], (a, above), has_above, recv + 6)
+            return [copy(mid.at[num], got_mid.at[num], (a, above), has_above, recv + 6)]
 
         def send_far(self):
             t, num, mine, recv = self.t, self.t.number, q[self.t.number], self.recv
@@ -252,7 +264,9 @@
 
         def sides(self):
             t, num, mine, recv = self.t, self.t.number, q[self.t.number], self.recv
-            for n, (i, j) in list(enumerate(t.down))[1:]:
+            for n, (i, j) in enumerate(t.down):
+                if (i, j) == (1, 1):
+                    continue
                 when(has_above, arrival(got_down.at[num * 3 + n], recv + 1 + n).wait_recv)
                 self.put((i + 1, j + 1), mine[t.at(i + 1, j + 1)] + got_down[num * 3 + n])
             for n, (i, j) in enumerate(t.up):
@@ -273,8 +287,9 @@
             when(has_below, arrival(got_far_up.at[num], recv + 7).wait_recv)
             self.put((0, 0), mine[t.at(0, 0)] + got_far_up[num])
 
-    t0, t1, t2 = TYPES
+    t0, t1, t2, t3 = TYPES
     pair_right = Gather(t1, LEFT_PAIR, right, last_half)
+    pair_left = Gather(t3, OWN_PAIR, left, first_half)
     rows_right = Gather(t0, LEFT_ROWS, right, last_half)
     rows_left = Gather(t0, RIGHT_ROWS, left, first_half)
 
@@ -283,7 +298,9 @@
         rows_left.send(key)
 
     line0, line1, line2 = Line(t0, rows_done), Line(t1, pair_right.send), Line(t2, lambda key: None)
+    line3 = Line(t3, pair_left.send)
     lc = Reduce(send_lc, got_lc, t1, left, first_half, last_half)
+    cr = Reduce(send_cr, got_cr, t3, right, last_half, first_half)
     ll = Reduce(send_ll, got_ll, t0, left, first_half, last_half)
     rr = Reduce(send_rr, got_rr, t0, right, last_half, first_half)
 
@@ -298,55 +315,79 @@
     loads[0].wait()
     weigh(0)
     loads[1].wait()
-    product(0, 2, q2, False)
+    product(0, 2, (t2, q2))
+    pl.semaphore_wait(barrier, peers)
     for key in in_order(t2):
         line2.start(key)
-    product(0, 0, send_ll, True)
+    product(0, 0, (t0, send_ll))
     for key in in_order(t0):
         ll.send(key)
     loads[2].wait()
-    product(0, 1, send_lc, False)
+    product(0, 1, (t1, send_lc), (t3, q3))
     for key in in_order(t1):
         lc.send(key)
     weigh(2)
-    product(2, 2, send_rr, True)
+    product(2, 2, (t0, send_rr))
     for key in in_order(t0):
         rr.send(key)
     weigh(1)
-    product(1, 1, q0, True)
-    product(1, 2, q1, False)
+    product(1, 2, (t1, q1), (t3, send_cr))
+    for key in in_order(t3):
+        cr.send(key)
+    product(1, 1, (t0, q0))
     line2.send_far()
-    for key in in_order(t0):
+    first = []
+    for key in ((0, 0), (1, 1)):
         ll.add(key, q0)
         rr.add(key, q0)
-        line0.start(key)
-    for key in in_order(t1):
+        first += line0.start(key)
+    for key in ((0, 0), (1, 1)):
         lc.add(key, q1)
-        line1.start(key)
-    line0.send_mid()
+        first += line1.start(key)
+    for key in ((2, 2), (0, 1), (1, 2), (0, 2)):
+        ll.add(key, q0)
+        rr.add(key, q0)
+    middle = line0.send_mid()
+    for key in ((2, 2), (0, 2), (2, 0)):
+        lc.add(key, q1)
+    middle += line1.send_mid()
+    line0.start((0, 2))
+    line1.start((0, 2))
+    line1.start((2, 0))
+    for key in in_order(t3):
+        cr.add(key, q3)
+    flush(first)
+    sides = []
+    for key in ((0, 1), (1, 2)):
+        sides += line0.start(key)
+    for key in ((0, 1), (1, 0)):
+        sides += line3.start(key)
     line0.send_far()
-    line1.send_mid()
+    line1.send_far()
+    line0.high()
+    line1.high()
+    flush(middle)
+    for key in ((1, 2), (2, 1)):
+        line3.start(key)
+    line0.centre()
+    line1.centre()
+    line0.low()
+    line1.low()
+    flush(sides)
     line2.send_mid()
     line0.sides()
-    line0.high()
-    line1.send_far()
-    line1.sides()
-    line1.high()
-    line0.centre()
-    line0.low()
-    line1.centre()
-    line1.low()
+    line3.sides()
     line2.sides()
     line2.high()
     line2.centre()
     line2.low()
-    for gather in (pair_right, rows_right, rows_left):
+    for gather in (pair_right, pair_left, rows_right, rows_left):
         gather.wait()
     for c, exists in sent:
         when(exists, c.wait_send)
 
 
-COPIES = 96
+COPIES = 128
 
 
 def exchange(values, potential, n_atoms, n_grid):
@@ -361,8 +402,8 @@
         out_specs=vmem,
         scratch_shapes=[
             pltpu.VMEM((3 * B, values.shape[0]), BF16),
-            blocks(6), blocks(6), blocks(9), blocks(6), blocks(9), blocks(9),
-            blocks(7), blocks(7), blocks(10), blocks(9), blocks(6), blocks(3), blocks(3), blocks(3), blocks(3), blocks(3),
+            blocks(6), blocks(6), blocks(9), blocks(9), blocks(6), blocks(9), blocks(9), blocks(9),
+            blocks(7), blocks(7), blocks(10), blocks(10), blocks(12), blocks(8), blocks(3), blocks(3), blocks(3), blocks(3), blocks(3),
             pltpu.VMEM(values.shape, BF16),
             pltpu.SemaphoreType.DMA((COPIES,)),
             pltpu.SemaphoreType.DMA((COPIES,)),

time: 52.6 us -> 49.9 us (0.949)
  the two profiles are of different devices: /device:TPU:8 before, /device:TPU:201 now
where the time goes in v4:
time: 49.9 us; the launch traced here: 49.8 us
  Pallas kernels  49 us (98%)
  local copies, waits for them, and re-layouts  0.71 us (1%)
    pallas_call x1, Pallas kernels, exchange(): pl.pallas_call(lambda *refs: exchange_kernel(n_atoms, n_grid, *refs), out...  41.8 us
    pallas_call x1, Pallas kernels, sign_columns(): pl.pallas_call(sign_kernel, out_shape=jax.ShapeDtypeStruct((n, B), F32),...  7.28 us

profile of v4, /device:TPU:201, one launch (start us, length us, event | category | flops | bytes accessed | tf_op | source)
XLA Modules:
  0.0 49.8 jit_solution(14449277811282091422)
XLA Ops:
  0.0 0.0 copy-start.1
  0.0 0.0 copy-start
  0.0 0.7 %copy-done = f32[1,1,2048]{2,1,0:T(1,128)S(1)} copy-done((f32[1,1,2048]{2,1,0:T(1,128)S(1)}, f32[1,1,2048]{2,1,0:T(1,128)}, u32[]{:S(2)}) %copy-start) | copy-done | bytes 8216
  0.7 41.8 %exchange.1.blocks = f32[45,128,128]{2,1,0:T(8,128)S(1)} custom-call(bf16[2048,1152]{1,0:T(8,128)(2,1)} %bitcast.6, f32[1,2048]{1,0:T(1,128)S(1)} %bitcast.4), custom_call_target="tpu_custom_call" | custom-call | tf_op jit(solution)/shard_map/exchange/pallas_call | solution.py:398
  42.5 0.0 copy-done.1
  42.5 7.3 %sign_columns.1 = f32[768,128]{1,0:T(8,128)} custom-call(s32[6]{0:T(128)S(1)} %bitcast.5, f32[45,128,128]{2,1,0:T(8,128)S(1)} %exchange.1.blocks), custom_call_target="tpu_custom_call" | custom-call | tf_op jit(solution)/shard_map/sign_columns/pallas_call | solution.py:509
Async XLA Ops:
  0.0 42.5 %copy-start.1 = (s32[1,1,6]{2,1,0:T(1,128)S(1)}, s32[1,1,6]{2,1,0:T(1,128)}, u32[]{:S(2)}) copy-start(s32[1,1,6]{2,1,0:T(1,128)} %param.5) | copy-start | bytes 76
  0.0 0.7 %copy-start = (f32[1,1,2048]{2,1,0:T(1,128)S(1)}, f32[1,1,2048]{2,1,0:T(1,128)}, u32[]{:S(2)}) copy-start(f32[1,1,2048]{2,1,0:T(1,128)} %param.4) | copy-start | bytes 24580

commit v5 on v4

--- a/solution.py
+++ b/solution.py
@@ -369,12 +369,11 @@
     flush(middle)
     for key in ((1, 2), (2, 1)):
         line3.start(key)
+    line2.send_mid()
     line0.centre()
     line1.centre()
     line0.low()
     line1.low()
-    flush(sides)
-    line2.send_mid()
     line0.sides()
     line3.sides()
     line2.sides()

time: 49.9 us -> 49.4 us (0.990)
  the two profiles are of different devices: /device:TPU:201 before, /device:TPU:8 now
where the time goes in v5:
time: 49.4 us; the launch traced here: 48.6 us
  Pallas kernels  47.9 us (97%)
  local copies, waits for them, and re-layouts  0.71 us (1%)
    pallas_call x1, Pallas kernels, exchange(): pl.pallas_call(lambda *refs: exchange_kernel(n_atoms, n_grid, *refs), out...  40.6 us
    pallas_call x1, Pallas kernels, sign_columns(): pl.pallas_call(sign_kernel, out_shape=jax.ShapeDtypeStruct((n, B), F32),...  7.27 us

profile of v5, /device:TPU:8, one launch (start us, length us, event | category | flops | bytes accessed | tf_op | source)
XLA Modules:
  0.0 48.6 jit_solution(8544709333305636492)
XLA Ops:
  0.0 0.0 copy-start.1
  0.0 0.0 copy-start
  0.0 0.7 %copy-done = f32[1,1,2048]{2,1,0:T(1,128)S(1)} copy-done((f32[1,1,2048]{2,1,0:T(1,128)S(1)}, f32[1,1,2048]{2,1,0:T(1,128)}, u32[]{:S(2)}) %copy-start) | copy-done | bytes 8216
  0.7 40.6 %exchange.1.blocks = f32[45,128,128]{2,1,0:T(8,128)S(1)} custom-call(bf16[2048,1152]{1,0:T(8,128)(2,1)} %bitcast.6, f32[1,2048]{1,0:T(1,128)S(1)} %bitcast.4), custom_call_target="tpu_custom_call" | custom-call | tf_op jit(solution)/shard_map/exchange/pallas_call | solution.py:397
  41.4 0.0 copy-done.1
  41.4 7.3 %sign_columns.1 = f32[768,128]{1,0:T(8,128)} custom-call(s32[6]{0:T(128)S(1)} %bitcast.5, f32[45,128,128]{2,1,0:T(8,128)S(1)} %exchange.1.blocks), custom_call_target="tpu_custom_call" | custom-call | tf_op jit(solution)/shard_map/sign_columns/pallas_call | solution.py:508
Async XLA Ops:
  0.0 41.4 %copy-start.1 = (s32[1,1,6]{2,1,0:T(1,128)S(1)}, s32[1,1,6]{2,1,0:T(1,128)}, u32[]{:S(2)}) copy-start(s32[1,1,6]{2,1,0:T(1,128)} %param.5) | copy-start | bytes 76
  0.0 0.7 %copy-start = (f32[1,1,2048]{2,1,0:T(1,128)S(1)}, f32[1,1,2048]{2,1,0:T(1,128)}, u32[]{:S(2)}) copy-start(f32[1,1,2048]{2,1,0:T(1,128)} %param.4) | copy-start | bytes 24580

commit v6 on v5

--- a/solution.py
+++ b/solution.py
@@ -319,13 +319,13 @@
     pl.semaphore_wait(barrier, peers)
     for key in in_order(t2):
         line2.start(key)
-    product(0, 0, (t0, send_ll))
-    for key in in_order(t0):
-        ll.send(key)
     loads[2].wait()
     product(0, 1, (t1, send_lc), (t3, q3))
     for key in in_order(t1):
         lc.send(key)
+    product(0, 0, (t0, send_ll))
+    for key in in_order(t0):
+        ll.send(key)
     weigh(2)
     product(2, 2, (t0, send_rr))
     for key in in_order(t0):

time: 49.4 us -> 48.4 us (0.980)
  Pallas kernels: 47.9 us -> 47 us
    pallas_call x1, Pallas kernels: 40.6 us -> 39.7 us  [exchange(): pl.pallas_call(lambda *refs: exchange_kernel(n_atoms, n_grid, *refs), out...]
where the time goes in v6:
time: 48.4 us; the launch traced here: 47.7 us
  Pallas kernels  47 us (97%)
  local copies, waits for them, and re-layouts  0.71 us (1%)
    pallas_call x1, Pallas kernels, exchange(): pl.pallas_call(lambda *refs: exchange_kernel(n_atoms, n_grid, *refs), out...  39.7 us
    pallas_call x1, Pallas kernels, sign_columns(): pl.pallas_call(sign_kernel, out_shape=jax.ShapeDtypeStruct((n, B), F32),...  7.26 us

profile of v6, /device:TPU:8, one launch (start us, length us, event | category | flops | bytes accessed | tf_op | source)
XLA Modules:
  0.0 47.7 jit_solution(17655379909357585313)
XLA Ops:
  0.0 0.0 copy-start.1
  0.0 0.0 copy-start
  0.0 0.7 %copy-done = f32[1,1,2048]{2,1,0:T(1,128)S(1)} copy-done((f32[1,1,2048]{2,1,0:T(1,128)S(1)}, f32[1,1,2048]{2,1,0:T(1,128)}, u32[]{:S(2)}) %copy-start) | copy-done | bytes 8216
  0.7 39.7 %exchange.1.blocks = f32[45,128,128]{2,1,0:T(8,128)S(1)} custom-call(bf16[2048,1152]{1,0:T(8,128)(2,1)} %bitcast.6, f32[1,2048]{1,0:T(1,128)S(1)} %bitcast.4), custom_call_target="tpu_custom_call" | custom-call | tf_op jit(solution)/shard_map/exchange/pallas_call | solution.py:397
  40.4 0.0 copy-done.1
  40.4 7.3 %sign_columns.1 = f32[768,128]{1,0:T(8,128)} custom-call(s32[6]{0:T(128)S(1)} %bitcast.5, f32[45,128,128]{2,1,0:T(8,128)S(1)} %exchange.1.blocks), custom_call_target="tpu_custom_call" | custom-call | tf_op jit(solution)/shard_map/sign_columns/pallas_call | solution.py:508
Async XLA Ops:
  0.0 40.4 %copy-start.1 = (s32[1,1,6]{2,1,0:T(1,128)S(1)}, s32[1,1,6]{2,1,0:T(1,128)}, u32[]{:S(2)}) copy-start(s32[1,1,6]{2,1,0:T(1,128)} %param.5) | copy-start | bytes 76
  0.0 0.7 %copy-start = (f32[1,1,2048]{2,1,0:T(1,128)S(1)}, f32[1,1,2048]{2,1,0:T(1,128)}, u32[]{:S(2)}) copy-start(f32[1,1,2048]{2,1,0:T(1,128)} %param.4) | copy-start | bytes 24580
